TPU v7x, 32 devices: a whole 2x2x4 slice. The times are simulated.
32 devices in a mesh: dp: 4 (over z), ctx: 8 (over y, x, core).
Axes of the slice: x: 2, y: 2, z: 4, core: 2. Of those that a mesh axis runs over, the one named last changes fastest.
Arguments:
- tokens: bfloat16 [4, 1024, 8192], P('dp', 'ctx'), may hold values from -6 to 6
- w_down: bfloat16 [8192, 512], P(('dp', 'ctx')), may hold values from -0.0625 to 0.0625
- w_up: bfloat16 [512, 1024], replicated, may hold values from -0.25 to 0.25
- queries: bfloat16 [4, 1024, 4096], P('dp', 'ctx'), may hold values from -70 to 70, as said below
- block_order: int32 [4, 16], P('dp', 'ctx'), may hold values from 0 to 15, each once within a row
Outputs:
- attended: bfloat16 [4, 1024, 4096], P('dp', 'ctx')
Inputs may be any that keep to these rules, and one draw needn't show every extreme that they name: `queries`: query entries.
All inputs are finite; a program needn't handle non-finite values.
Results may differ from a plain program's by a relative error of at most 0.014.
The roundings to bfloat16 on the way count: a program that leaves them out, or rounds other values in their place, can miss the bound.
Values may be sent and summed in bfloat16 or wider, within the bound.
A program may use at most 64 MiB of HBM per device.

v0:
```python
import math

import jax
import jax.numpy as jnp
from jax import lax
from jax.sharding import PartitionSpec as P

QH = 32
KVH = 4
HD = 128


def per_device(tokens, w_down, w_up, queries, block_order):
    local_rows = tokens.shape[1]
    half_rows = local_rows // 2
    features = tokens[0]
    summed = jnp.dot(
        features,
        lax.all_gather(w_down, ("dp", "ctx"), axis=0, tiled=True),
        preferred_element_type=jnp.float32,
    )
    latent = summed.astype(jnp.bfloat16)
    order_whole = lax.all_gather(block_order, "ctx", axis=1, tiled=True)[0]
    block_count = order_whole.shape[0]
    local_ids = jnp.arange(local_rows, dtype=jnp.int32)
    query_pos = (
        jnp.where(local_ids < half_rows, block_order[0, 0], block_order[0, 1]) * half_rows
        + local_ids % half_rows
    )
    group = QH // KVH
    query_heads = queries[0].reshape(local_rows, KVH, group, HD).transpose(1, 2, 0, 3)
    score_scale = HD ** (-0.5)

    def update(carry, kv_block, key_pos):
        running_max, running_total, running_sum = carry
        width = kv_block.shape[0]
        key_block = kv_block[:, : KVH * HD].reshape(width, KVH, HD)
        value_block = kv_block[:, KVH * HD :].reshape(width, KVH, HD)
        scores = (
            jnp.einsum("kgsd,tkd->kgst", query_heads, key_block, preferred_element_type=jnp.float32)
            * score_scale
        )
        allowed = key_pos[None, :] <= query_pos[:, None]
        scores = jnp.where(allowed, scores, -1e30)
        new_max = jnp.maximum(running_max, jnp.max(scores, axis=-1))
        correction = jnp.exp(running_max - new_max)
        expo = jnp.where(allowed, jnp.exp(scores - new_max[..., None]), 0.0)
        new_total = running_total * correction + jnp.sum(expo, axis=-1)
        contrib = jnp.einsum(
            "kgst,tkd->kgsd",
            expo.astype(jnp.bfloat16),
            value_block,
            preferred_element_type=jnp.float32,
        )
        return (new_max, new_total, running_sum * correction[..., None] + contrib)

    start_state = (
        jnp.full((KVH, group, local_rows), -1e30, jnp.float32),
        jnp.zeros((KVH, group, local_rows), jnp.float32),
        jnp.zeros((KVH, group, local_rows, HD), jnp.float32),
    )
    kv_local = jnp.dot(latent, w_up, preferred_element_type=jnp.float32).astype(jnp.bfloat16)
    piece = lax.all_gather(kv_local, "ctx", axis=0, tiled=True)
    count = piece.shape[0]
    width = math.gcd(count, 256)
    blocks = piece.reshape(count // width, width, piece.shape[1])
    row_ids = jnp.arange(count, dtype=jnp.int32)
    onehot = (row_ids // half_rows)[:, None] == jnp.arange(block_count, dtype=jnp.int32)[None, :]
    block_ids = jnp.sum(jnp.where(onehot, order_whole[None, :], 0), axis=1)
    key_positions = (block_ids * half_rows + row_ids % half_rows).reshape(count // width, width)

    def step_block(state, inputs):
        block, key_pos = inputs
        state = update(state, block, key_pos)
        return (state, None)

    result, unused = lax.scan(step_block, start_state, (blocks, key_positions))
    unused_max, final_total, final_sum = result
    outputs = final_sum / final_total[..., None]
    return outputs.transpose(2, 0, 1, 3).reshape(1, local_rows, QH * HD).astype(jnp.bfloat16)


def solution(mesh):
    placed = (
        P("dp", "ctx", None),
        P(("dp", "ctx"), None),
        P(),
        P("dp", "ctx", None),
        P("dp", "ctx"),
    )
    return jax.shard_map(
        per_device, mesh=mesh, in_specs=placed, out_specs=P("dp", "ctx", None), check_vma=False
    )
```

profile of v0, /device:TPU:1, one launch (start us, length us, event | category | flops | bytes accessed | tf_op | source)
XLA Modules:
  0.0 171.6 jit_solution(13662498133776428902)
XLA Ops:
  7.3 82.9 %all-gather.3.cloned.1.call-done = bf16[8192,512]{1,0:T(8,128)(2,1)} async-done(((bf16[256,512]{1,0:T(8,128)(2,1)}), bf16[8192,512]{1,0:T(8,128)(2,1)}) %all-gather.3.cloned.1.call-update) | async-done | bytes 8388624 | tf_op jit(solution)/shard_map/all_gather | solution.py:19
  90.2 5.8 %convolution_convert_fusion = bf16[128,1024]{1,0:T(8,128)(2,1)} fusion(bf16[512,1024]{1,0:T(8,128)(2,1)} %param.9, bf16[8192,512]{1,0:T(8,128)(2,1)} %all-gather.3.cloned.1.call-done, bf16[1,128,8192]{2,1,0:T(8,128)(2,1)S(1)} %copy-done), kind=kOutput, calls=%fused_computation.31 | convolution fusion | flops 1208156160 | bytes 11796480 | tf_op jit(solution)/shard_map/dot_general | solution.py:62
  97.5 5.3 %all-reduce = s32[16]{0:T(128)S(1)} all-reduce(s32[16]{0:T(128)S(1)} %bitcast_dynamic-update-slice_fusion), channel_id=1, replica_groups=mesh['dp'=4,'ctx'=8] {'ctx'}, use_global_device_ids=true, to_apply=%add | all-reduce | flops 16 | bytes 128
  102.9 1.6 copy.18
  104.5 1.3 copy.20
  106.5 16.3 %all-gather.5.cloned.1.call-done = bf16[1024,1024]{1,0:T(8,128)(2,1)} async-done(((bf16[128,1024]{1,0:T(8,128)(2,1)}), bf16[1024,1024]{1,0:T(8,128)(2,1)}) %all-gather.5.cloned.1.call-update) | async-done | bytes 2097168 | tf_op jit(solution)/shard_map/all_gather | solution.py:63
  122.7 38.1 %while.15 = (s32[]{:T(128)}, f32[4,8,128]{2,1,0:T(8,128)S(1)}, f32[4,8,128]{2,1,0:T(8,128)S(1)}, f32[4,8,128,128]{3,2,1,0:T(8,128)}, s32[4,256]{1,0:T(4,128)S(1)...) while((s32[]{:T(128)}, f32[4,8,128]{2,1,0:T(8,128)S(1)}, ...), condition=%wide.region_4.5_spmd.clone, body=%wide.region_1.4_spmd.clone.sunk | while | flops 552129792 | bytes 38670536 | solution.py:77
  122.7 1.3 fusion.55
  125.5 2.2 %fusion.57 = (f32[4,8,128]{2,1,0:T(8,128)S(1)}, f32[4,256,8,128]{3,1,2,0:T(8,128)S(1)}) fusion(pred[128,256]{0,1:T(8,128)(4,1)S(1)} %broadcast_compare_fusion.2, bf16[256,4,128,1]{0,2,3,1:T(8,128)(2,1)S(1)} %bitcast.71, bf16[4,8,128,128]{3,2,1,0:T(8,128)(2,1)} %get-tuple-element.223), kind=kOutput, calls=%fused_computation.3.clone.1 | convolution fusion | flops 271577088 | bytes 5554176 | tf_op jit(solution)/shard_map/while/body/eval_jaxpr/kgsd,tkd->kgst/dot_general | solution.py:40
  128.8 2.1 %fusion.60 = f32[4,8,128,128]{3,2,1,0:T(8,128)S(1)} fusion(f32[4,8,128,128]{3,2,1,0:T(8,128)S(1)} %copy-done.1, bf16[256,4,128,1]{0,2,3,1:T(8,128)(2,1)S(1)} %bitcast.72, f32[4,256,8,128]{3,1,2,0:T(8,128)S(1)} %get-tuple-element.191, f32[4,8,128]{2,1,0:T(8,128)S(1)} %select_maximum_fusion.2, pred[128,256]{0,1:T(8,128)(4,1)S(1)} %broadcast_compare_fusion.2, ...), kind=kOutput, calls=%fused_computation.8.clone.1 | convolution fusion | flops 275251200 | bytes 8716289 | tf_op jit(solution)/shard_map/while/body/eval_jaxpr/kgst,tkd->kgsd/dot_general | solution.py:49
  131.0 1.3 copy-done.2
  132.3 1.3 fusion.55
  135.0 2.2 %fusion.57 = (f32[4,8,128]{2,1,0:T(8,128)S(1)}, f32[4,256,8,128]{3,1,2,0:T(8,128)S(1)}) fusion(pred[128,256]{0,1:T(8,128)(4,1)S(1)} %broadcast_compare_fusion.2, bf16[256,4,128,1]{0,2,3,1:T(8,128)(2,1)S(1)} %bitcast.71, bf16[4,8,128,128]{3,2,1,0:T(8,128)(2,1)} %get-tuple-element.223), kind=kOutput, calls=%fused_computation.3.clone.1 | convolution fusion | flops 271577088 | bytes 5554176 | tf_op jit(solution)/shard_map/while/body/eval_jaxpr/kgsd,tkd->kgst/dot_general | solution.py:40
  138.4 2.1 %fusion.60 = f32[4,8,128,128]{3,2,1,0:T(8,128)S(1)} fusion(f32[4,8,128,128]{3,2,1,0:T(8,128)S(1)} %copy-done.1, bf16[256,4,128,1]{0,2,3,1:T(8,128)(2,1)S(1)} %bitcast.72, f32[4,256,8,128]{3,1,2,0:T(8,128)S(1)} %get-tuple-element.191, f32[4,8,128]{2,1,0:T(8,128)S(1)} %select_maximum_fusion.2, pred[128,256]{0,1:T(8,128)(4,1)S(1)} %broadcast_compare_fusion.2, ...), kind=kOutput, calls=%fused_computation.8.clone.1 | convolution fusion | flops 275251200 | bytes 8716289 | tf_op jit(solution)/shard_map/while/body/eval_jaxpr/kgst,tkd->kgsd/dot_general | solution.py:49
  140.5 1.3 copy-done.2
  141.8 1.3 fusion.55
  144.6 2.2 %fusion.57 = (f32[4,8,128]{2,1,0:T(8,128)S(1)}, f32[4,256,8,128]{3,1,2,0:T(8,128)S(1)}) fusion(pred[128,256]{0,1:T(8,128)(4,1)S(1)} %broadcast_compare_fusion.2, bf16[256,4,128,1]{0,2,3,1:T(8,128)(2,1)S(1)} %bitcast.71, bf16[4,8,128,128]{3,2,1,0:T(8,128)(2,1)} %get-tuple-element.223), kind=kOutput, calls=%fused_computation.3.clone.1 | convolution fusion | flops 271577088 | bytes 5554176 | tf_op jit(solution)/shard_map/while/body/eval_jaxpr/kgsd,tkd->kgst/dot_general | solution.py:40
  147.9 2.1 %fusion.60 = f32[4,8,128,128]{3,2,1,0:T(8,128)S(1)} fusion(f32[4,8,128,128]{3,2,1,0:T(8,128)S(1)} %copy-done.1, bf16[256,4,128,1]{0,2,3,1:T(8,128)(2,1)S(1)} %bitcast.72, f32[4,256,8,128]{3,1,2,0:T(8,128)S(1)} %get-tuple-element.191, f32[4,8,128]{2,1,0:T(8,128)S(1)} %select_maximum_fusion.2, pred[128,256]{0,1:T(8,128)(4,1)S(1)} %broadcast_compare_fusion.2, ...), kind=kOutput, calls=%fused_computation.8.clone.1 | convolution fusion | flops 275251200 | bytes 8716289 | tf_op jit(solution)/shard_map/while/body/eval_jaxpr/kgst,tkd->kgsd/dot_general | solution.py:49
  150.0 1.3 copy-done.2
  151.3 1.3 fusion.55
  154.1 2.2 %fusion.57 = (f32[4,8,128]{2,1,0:T(8,128)S(1)}, f32[4,256,8,128]{3,1,2,0:T(8,128)S(1)}) fusion(pred[128,256]{0,1:T(8,128)(4,1)S(1)} %broadcast_compare_fusion.2, bf16[256,4,128,1]{0,2,3,1:T(8,128)(2,1)S(1)} %bitcast.71, bf16[4,8,128,128]{3,2,1,0:T(8,128)(2,1)} %get-tuple-element.223), kind=kOutput, calls=%fused_computation.3.clone.1 | convolution fusion | flops 271577088 | bytes 5554176 | tf_op jit(solution)/shard_map/while/body/eval_jaxpr/kgsd,tkd->kgst/dot_general | solution.py:40
  157.4 2.1 %fusion.60 = f32[4,8,128,128]{3,2,1,0:T(8,128)S(1)} fusion(f32[4,8,128,128]{3,2,1,0:T(8,128)S(1)} %copy-done.1, bf16[256,4,128,1]{0,2,3,1:T(8,128)(2,1)S(1)} %bitcast.72, f32[4,256,8,128]{3,1,2,0:T(8,128)S(1)} %get-tuple-element.191, f32[4,8,128]{2,1,0:T(8,128)S(1)} %select_maximum_fusion.2, pred[128,256]{0,1:T(8,128)(4,1)S(1)} %broadcast_compare_fusion.2, ...), kind=kOutput, calls=%fused_computation.8.clone.1 | convolution fusion | flops 275251200 | bytes 8716289 | tf_op jit(solution)/shard_map/while/body/eval_jaxpr/kgst,tkd->kgsd/dot_general | solution.py:49
  159.6 1.3 copy-done.2
  160.8 1.9 %fusion.28 = bf16[128,4,8,128]{3,0,2,1:T(8,128)(2,1)S(1)} fusion(f32[4,8,128,128]{3,2,1,0:T(8,128)} %get-tuple-element.48, f32[4,8,128]{2,1,0:T(8,128)S(1)} %get-tuple-element.49), kind=kLoop, calls=%fused_computation.33 | loop fusion | flops 1048576 | bytes 3162112 | tf_op jit(solution)/shard_map/convert_element_type | solution.py:80
  (72 shorter events, 14.3 us)
Async XLA Ops:
  6.5 83.7 %copy-start = (bf16[1,128,8192]{2,1,0:T(8,128)(2,1)S(1)}, bf16[1,128,8192]{2,1,0:T(8,128)(2,1)}, u32[]{:S(2)}) copy-start(bf16[1,128,8192]{2,1,0:T(8,128)(2,1)} %param.7) | copy-start | bytes 6291460
  6.5 83.7 %all-gather.3.cloned.1.call-start = ((), (), s32[]{:S(2)}) async-start(), calls=%async_computation | async-start | bytes 8650752 | tf_op jit(solution)/shard_map/all_gather | solution.py:19
  7.3 88.8 %copy-start.4 = (u32[32]{0:T(128)S(1)}, u32[32]{0:T(128)}, u32[]{:S(2)}) copy-start(u32[32]{0:T(128)} %constant.71) | copy-start | bytes 388
  7.3 90.1 %copy-start.3 = (s32[1,2]{1,0:T(1,128)S(1)}, s32[1,2]{1,0:T(1,128)}, u32[]{:S(2)}) copy-start(s32[1,2]{1,0:T(1,128)} %param.11) | copy-start | bytes 28
  7.3 115.5 %all-gather.5.cloned.1.call-start = ((), (), s32[]{:S(2)}) async-start(), calls=%async_computation.1 | async-start | bytes 2359296 | tf_op jit(solution)/shard_map/all_gather | solution.py:63
  125.5 3.3 %copy-start.1 = (f32[4,8,128,128]{3,2,1,0:T(8,128)S(1)}, f32[4,8,128,128]{3,2,1,0:T(8,128)}, u32[]{:S(2)}) copy-start(f32[4,8,128,128]{3,2,1,0:T(8,128)} %get-tuple-element.209) | copy-start | bytes 6291460 | tf_op jit(solution)/shard_map/while
  131.0 1.3 copy-start.2
  135.0 3.3 %copy-start.1 = (f32[4,8,128,128]{3,2,1,0:T(8,128)S(1)}, f32[4,8,128,128]{3,2,1,0:T(8,128)}, u32[]{:S(2)}) copy-start(f32[4,8,128,128]{3,2,1,0:T(8,128)} %get-tuple-element.209) | copy-start | bytes 6291460 | tf_op jit(solution)/shard_map/while
  140.5 1.3 copy-start.2
  144.5 3.3 %copy-start.1 = (f32[4,8,128,128]{3,2,1,0:T(8,128)S(1)}, f32[4,8,128,128]{3,2,1,0:T(8,128)}, u32[]{:S(2)}) copy-start(f32[4,8,128,128]{3,2,1,0:T(8,128)} %get-tuple-element.209) | copy-start | bytes 6291460 | tf_op jit(solution)/shard_map/while
  150.0 1.3 copy-start.2
  154.1 3.3 %copy-start.1 = (f32[4,8,128,128]{3,2,1,0:T(8,128)S(1)}, f32[4,8,128,128]{3,2,1,0:T(8,128)}, u32[]{:S(2)}) copy-start(f32[4,8,128,128]{3,2,1,0:T(8,128)} %get-tuple-element.209) | copy-start | bytes 6291460 | tf_op jit(solution)/shard_map/while
  159.5 1.3 copy-start.2
Sparse Core Ops, SparseCore 0:
  10.2 79.9 all-gather.2
  96.2 26.4 all-gather.4
where the time goes:
time: 172 us
  waiting for transfers between devices  99.9 us (58%)
  matrix products  23.1 us (13%)
  local copies, waits for them, and re-layouts  16.7 us (10%)
  between operations  14.1 us (8%)
  other arithmetic  12 us (7%)
  blocking collectives  5.31 us (3%)
    all_gather x1, waiting for transfers between devices, per_device(): lax.all_gather(w_down, ('dp', 'ctx'), axis=0, tiled=True)  82.9 us
    all_gather x1, waiting for transfers between devices, per_device(): piece = lax.all_gather(kv_local, 'ctx', axis=0, tiled=True)  16.3 us
    dot_general x4, matrix products, update(): jnp.einsum('kgsd,tkd->kgst', query_heads, key_block, preferred_element_ty...  8.83 us
    dot_general x4, matrix products, update(): jnp.einsum('kgst,tkd->kgsd', expo.astype(jnp.bfloat16), value_block, pref...  8.43 us
    dot_general x1, matrix products, per_device(): jnp.dot(latent, w_up, preferred_element_type=jnp.float32)  5.85 us
    unnamed x1, blocking collectives  5.31 us
    dynamic_slice x12, local copies, waits for them, and re-layouts, per_device(): result, unused = lax.scan(step_block, start_state, (blocks, key_positions))  5.19 us
    while x20, local copies, waits for them, and re-layouts  5.18 us
  transfers between devices with their start and end apart: 2, of which 2 were waited for; matrix products, arithmetic and copies ran while one was open for 3% of the time, Pallas kernels for 0%

commit v1 on v0

v1 whole, which is shorter than its diff:
```python
import functools
import math

import jax
import jax.numpy as jnp
from jax import lax
from jax.experimental import pallas as pl
from jax.experimental.pallas import tpu as pltpu
from jax.sharding import PartitionSpec as P

QH = 32
KVH = 4
HD = 128
MESH = pl.DeviceIdType.MESH


def attention_kernel(order_ref, pos_ref, latent_ref, w_up_ref, q_ref, out_ref, kv, bias):
    rows = q_ref.shape[1]
    count = latent_ref.shape[0]
    half = rows // 2
    tile = math.gcd(count, 256)

    @pl.loop(0, count // tile)
    def _(i):
        part = pl.ds(pl.multiple_of(i * tile, tile), tile)
        kv[part, :] = jnp.dot(
            latent_ref[part, :], w_up_ref[...], preferred_element_type=jnp.float32
        ).astype(jnp.bfloat16)

    ids = lax.broadcasted_iota(jnp.int32, (rows, 1), 0)
    query_pos = jnp.where(ids < half, order_ref[0, 0], order_ref[0, 1]) * half + ids % half
    bias[...] = jnp.where(pos_ref[0:1, :] <= query_pos, 0.0, -1e30)
    scale = HD ** (-0.5) * math.log2(math.e)
    heads = 2
    group = QH // KVH

    def step(i):
        def cols(first, width):
            return pl.ds(pl.multiple_of(first * HD, HD), width * HD)

        g = i * heads // group
        queries = jnp.concatenate(
            [q_ref[0, :, cols(i * heads + k, 1)] for k in range(heads)], axis=0
        )
        scores = lax.dot_general(
            queries, kv[:, cols(g, 1)], (((1,), (1,)), ((), ())), preferred_element_type=jnp.float32
        )
        parts, totals = [], []
        for k in range(heads):
            kept = scores[k * rows : (k + 1) * rows] * scale + bias[...]
            largest = jnp.max(kept, axis=1, keepdims=True)
            expo = jnp.exp2(kept - largest)
            totals.append(jnp.sum(expo, axis=1, keepdims=True))
            parts.append(expo.astype(jnp.bfloat16))
        summed = jnp.dot(
            jnp.concatenate(parts, axis=0), kv[:, cols(KVH + g, 1)], preferred_element_type=jnp.float32
        )
        for k in range(heads):
            out_ref[0, :, cols(i * heads + k, 1)] = (
                summed[k * rows : (k + 1) * rows] / totals[k]
            ).astype(jnp.bfloat16)

    pairs = QH // heads
    together = 4 if count <= 1024 else 1

    @pl.loop(0, pairs // together)
    def _(i):
        for k in range(together):
            step(i * together + k)


def attend(block_order, positions, latent, w_up, queries):
    count = latent.shape[0]
    rows = queries.shape[1]
    vmem = pl.BlockSpec(memory_space=pltpu.VMEM)
    return pl.pallas_call(
        attention_kernel,
        out_shape=jax.ShapeDtypeStruct(queries.shape, jnp.bfloat16),
        in_specs=[pl.BlockSpec(memory_space=pltpu.SMEM), vmem, vmem, vmem, vmem],
        out_specs=vmem,
        scratch_shapes=[
            pltpu.VMEM((count, w_up.shape[1]), jnp.bfloat16),
            pltpu.VMEM((rows, count), jnp.float32),
        ],
        compiler_params=pltpu.CompilerParams(vmem_limit_bytes=48 * 2**20),
        name="attention",
    )(block_order, positions, latent, w_up, queries)


def latent_kernel(
    layers, order_ref, tokens_ref, w_ref, latent_ref, pos_ref,
    tok, w, acc, share, mine, gathered, pos_mine, pos_all,
    load_sem, own_sem, tok_send, tok_recv, w_send, w_recv, piece_recv,
    pos_send, pos_recv, sum_sem, lat_send, lat_recv, store_sem,
):
    plane = 8
    z, ctx = lax.axis_index("dp"), lax.axis_index("ctx")
    core, x, y = ctx % 2, ctx // 2 % 2, ctx // 4
    mate = ctx + 1 - 2 * core
    x_dev, y_dev = ctx + 2 - 4 * x, ctx + 4 - 8 * y
    p, px, py = y * 2 + x, y * 2 + 1 - x, (1 - y) * 2 + x
    pd = (1 - y) * 2 + 1 - x
    rows, depth, width = tokens_ref.shape[1], w_ref.shape[0], w_ref.shape[1]
    chunks = layers * 4
    quarter = depth // 4
    own = z * 4 + p

    def columns(j, side):
        return pl.ds(pl.multiple_of((j * 2 + side) * depth, depth), depth)

    def load(j):
        return pltpu.make_async_copy(
            tokens_ref.at[0, :, columns(j, core)], tok.at[j, pl.ds(0, rows), :], load_sem.at[j]
        )

    def swap(j):
        return pltpu.make_async_remote_copy(
            tokens_ref.at[0, :, columns(j, 1 - core)], tok.at[j, pl.ds(rows, rows), :],
            tok_send.at[j], tok_recv.at[j], device_id=(z, mate), device_id_type=MESH,
        )

    own_load = pltpu.make_async_copy(w_ref, w.at[own], own_sem)
    own_load.start()

    barrier = pltpu.get_barrier_semaphore()
    for d in range(1, plane):
        pl.semaphore_signal(barrier, inc=1, device_id=(z, (ctx + d) % plane), device_id_type=MESH)

    @pl.when(z > 0)
    def _():
        pl.semaphore_signal(barrier, inc=1, device_id=(z - 1, ctx), device_id_type=MESH)

    @pl.when(z < layers - 1)
    def _():
        pl.semaphore_signal(barrier, inc=1, device_id=(z + 1, ctx), device_id_type=MESH)

    edge = layers - 1
    along = (z + edge - 1) // edge + (edge - z + edge - 1) // edge
    pl.semaphore_wait(barrier, plane - 1 + along)

    sent = []

    def send(conds, src, dst, sem, device):
        index = len(sent)

        def copy():
            return pltpu.make_async_remote_copy(
                src, dst, w_send.at[index], sem, device_id=device, device_id_type=MESH
            )

        sent.append((conds, copy))
        when(conds, lambda: copy().start())

    def when(conds, body):
        if not conds:
            body()
        elif len(conds) == 1:
            pl.when(conds[0])(body)
        else:
            pl.when(jnp.logical_and(conds[0], conds[1]))(body)

    def arrived(dst, sem):
        pltpu.make_async_remote_copy(
            dst, dst, w_send.at[0], sem, device_id=(z, mate), device_id_type=MESH
        ).wait_recv()

    def multiply(j):
        acc[...] += jnp.dot(tok[j], w[j], preferred_element_type=jnp.float32)

    def inside(layer):
        return jnp.logical_and(layer >= 0, layer < layers)

    def sources(t):
        if t == 0:
            return [(0, z, [])]
        return [(s, z + s * t, [inside(z + s * t)]) for s in (-1, 1)]

    def ahead(s):
        return [1, -1] if s == 0 else [-s]

    def piece(j, q):
        return w.at[j, pl.ds(q * quarter, quarter), :]

    def column(t):
        for s, layer, conds in sources(t):
            j = layer * 4 + p
            block = w_ref if t == 0 else w.at[j]
            if t:
                when(conds, lambda: arrived(w.at[j], w_recv.at[j]))
            for step in ahead(s):
                send(conds + [inside(z + step)], block, w.at[j], w_recv.at[j], (z + step, ctx))
            send(conds, block, w.at[j], w_recv.at[j], (z, x_dev))
            send(conds, block, w.at[j], w_recv.at[j], (z, y_dev))
            if t:
                when(conds, lambda: multiply(j))

    def sides(t):
        for s, layer, conds in sources(t):
            for place, device, first in ((px, y_dev, 0), (py, x_dev, 1)):
                j = layer * 4 + place
                when(conds, lambda: arrived(w.at[j], w_recv.at[j]))
                for q in (first + 2, first) if t == 0 else (first,):
                    send(conds, piece(j, q), piece(j, q), piece_recv.at[layer, q], (z, device))
            for place in (px, py):
                when(conds, lambda: multiply(layer * 4 + place))

    def corner(t):
        for s, layer, conds in sources(t):
            j = layer * 4 + pd
            for q in (2, 3):
                when(conds, lambda: arrived(piece(j, q), piece_recv.at[layer, q]))
                for step in ahead(s):
                    send(
                        conds + [inside(z + step)], piece(j, q), piece(j, q), piece_recv.at[layer, q],
                        (z + step, ctx),
                    )
            for q in (0, 1):
                when(conds, lambda: arrived(piece(j, q), piece_recv.at[layer, q]))
            when(conds, lambda: multiply(j))

    column(0)

    def start_tokens(j, unused):
        swap(j).start()
        load(j).start()
        return unused

    lax.fori_loop(0, chunks, start_tokens, 0)

    half = rows // 2
    ids = lax.broadcasted_iota(jnp.int32, (8, rows), 1)
    pos_mine[...] = jnp.where(ids < half, order_ref[0, 0], order_ref[0, 1]) * half + ids % half

    def pos_slot(device):
        return pos_all.at[:, pl.ds(pl.multiple_of(device * rows, rows), rows)]

    def pos_copy(d):
        return pltpu.make_async_remote_copy(
            pos_mine, pos_slot(ctx), pos_send.at[d], pos_recv.at[ctx],
            device_id=(z, (ctx + d) % plane), device_id_type=MESH,
        )

    for d in range(1, plane):
        pos_copy(d).start()
    pos_all[:, pl.ds(pl.multiple_of(ctx * rows, rows), rows)] = pos_mine[...]

    def wait_tokens(j, unused):
        load(j).wait()
        swap(j).wait()
        return unused

    lax.fori_loop(0, chunks, wait_tokens, 0)
    own_load.wait()
    acc[...] = jnp.dot(tok[own], w[own], preferred_element_type=jnp.float32)

    for t in range(layers + 2):
        if 1 <= t < layers:
            column(t)
        if 0 <= t - 1 < layers:
            sides(t - 1)
        if 0 <= t - 2 < layers:
            corner(t - 2)

    total = pltpu.make_async_remote_copy(
        acc.at[pl.ds(rows, rows), :], share, sum_sem.at[0], sum_sem.at[1],
        device_id=(z, mate), device_id_type=MESH,
    )
    total.start()
    for conds, copy in sent:
        when(conds, lambda: copy().wait_send())
    for d in range(1, plane):
        pos_copy(d).wait_send()
        sender = (ctx + d) % plane
        pltpu.make_async_remote_copy(
            pos_mine, pos_slot(sender), pos_send.at[d], pos_recv.at[sender],
            device_id=(z, mate), device_id_type=MESH,
        ).wait_recv()
    pos_store = pltpu.make_async_copy(pos_all, pos_ref, store_sem.at[plane])
    pos_store.start()
    total.wait()
    mine[...] = (acc[0:rows, :] + share[...]).astype(jnp.bfloat16)

    part = rows // 2

    def block(device, first=0, size=rows):
        return gathered.at[pl.ds(pl.multiple_of(device * rows + first, part), size), :]

    lat_sent = []

    def lat_send_to(src, dst, recv, device):
        copy = pltpu.make_async_remote_copy(
            src, dst, lat_send.at[len(lat_sent)], lat_recv.at[recv], device_id=(z, device), device_id_type=MESH
        )
        copy.start()
        lat_sent.append(copy)

    def lat_arrived(dst, recv):
        pltpu.make_async_remote_copy(
            dst, dst, lat_send.at[0], lat_recv.at[recv], device_id=(z, mate), device_id_type=MESH
        ).wait_recv()

    stores = []

    def store(src, device, index):
        copy = pltpu.make_async_copy(
            src, latent_ref.at[pl.ds(pl.multiple_of(device * rows, rows), rows), :], store_sem.at[index]
        )
        copy.start()
        stores.append(copy)

    def partner(device):
        return device + 1 - 2 * core

    d_dev = pd * 2 + core
    lat_send_to(mine, block(ctx), 0, x_dev)
    lat_send_to(mine, block(ctx), 1, y_dev)
    lat_send_to(mine, block(ctx), 2, mate)
    store(mine, ctx, 0)
    lat_arrived(block(x_dev), 0)
    lat_send_to(block(x_dev, 0, part), block(x_dev, 0, part), 3, y_dev)
    lat_send_to(block(x_dev), block(x_dev), 5, mate)
    store(block(x_dev), x_dev, 1)
    lat_arrived(block(y_dev), 1)
    lat_send_to(block(y_dev, part, part), block(y_dev, part, part), 4, x_dev)
    lat_send_to(block(y_dev), block(y_dev), 6, mate)
    store(block(y_dev), y_dev, 2)
    lat_arrived(block(mate), 2)
    store(block(mate), mate, 3)
    lat_arrived(block(d_dev, 0, part), 3)
    lat_send_to(block(d_dev, 0, part), block(d_dev, 0, part), 7, mate)
    lat_arrived(block(d_dev, part, part), 4)
    lat_send_to(block(d_dev, part, part), block(d_dev, part, part), 8, mate)
    store(block(d_dev), d_dev, 4)
    lat_arrived(block(partner(x_dev)), 5)
    store(block(partner(x_dev)), partner(x_dev), 5)
    lat_arrived(block(partner(y_dev)), 6)
    store(block(partner(y_dev)), partner(y_dev), 6)
    lat_arrived(block(partner(d_dev), 0, part), 7)
    lat_arrived(block(partner(d_dev), part, part), 8)
    store(block(partner(d_dev)), partner(d_dev), 7)
    for copy in lat_sent:
        copy.wait_send()
    for copy in stores:
        copy.wait()
    pos_store.wait()


def gather_latent(layers, tokens, w_down, block_order):
    rows, features = tokens.shape[1], tokens.shape[2]
    depth, width = w_down.shape
    chunks = layers * 4
    dma = pltpu.SemaphoreType.DMA
    whole = pl.BlockSpec(memory_space=pl.ANY)
    return pl.pallas_call(
        functools.partial(latent_kernel, layers),
        out_shape=[
            jax.ShapeDtypeStruct((8 * rows, width), jnp.bfloat16),
            jax.ShapeDtypeStruct((8, 8 * rows), jnp.int32),
        ],
        in_specs=[pl.BlockSpec(memory_space=pltpu.SMEM), whole, whole],
        out_specs=[whole, whole],
        scratch_shapes=[
            pltpu.VMEM((chunks, 2 * rows, depth), jnp.bfloat16),
            pltpu.VMEM((chunks, depth, width), jnp.bfloat16),
            pltpu.VMEM((2 * rows, width), jnp.float32),
            pltpu.VMEM((rows, width), jnp.float32),
            pltpu.VMEM((rows, width), jnp.bfloat16),
            pltpu.VMEM((8 * rows, width), jnp.bfloat16),
            pltpu.VMEM((8, rows), jnp.int32),
            pltpu.VMEM((8, 8 * rows), jnp.int32),
            dma((chunks,)),
            dma,
            dma((chunks,)),
            dma((chunks,)),
            dma((96,)),
            dma((chunks,)),
            dma((layers, 4)),
            dma((8,)),
            dma((8,)),
            dma((2,)),
            dma((10,)),
            dma((9,)),
            dma((9,)),
        ],
        compiler_params=pltpu.CompilerParams(
            collective_id=0, has_side_effects=True, vmem_limit_bytes=48 * 2**20
        ),
        name="latent",
    )(block_order, tokens, w_down)


def per_device(layers, plane, tokens, w_down, w_up, queries, block_order):
    local_rows = tokens.shape[1]
    half_rows = local_rows // 2
    if plane == 8:
        latent, positions = gather_latent(layers, tokens, w_down, block_order)
        return attend(block_order, positions, latent, w_up, queries)
    summed = jnp.dot(
        tokens[0],
        lax.all_gather(w_down, ("dp", "ctx"), axis=0, tiled=True),
        preferred_element_type=jnp.float32,
    )
    latent = lax.all_gather(summed.astype(jnp.bfloat16), "ctx", axis=0, tiled=True)
    order = lax.all_gather(block_order, "ctx", axis=1, tiled=True)
    positions = jnp.repeat(order, half_rows, axis=1) * half_rows + jnp.tile(
        jnp.arange(half_rows, dtype=jnp.int32), order.shape[1]
    )
    return attend(block_order, positions, latent, w_up, queries)


def solution(mesh):
    placed = (
        P("dp", "ctx", None),
        P(("dp", "ctx"), None),
        P(),
        P("dp", "ctx", None),
        P("dp", "ctx"),
    )
    sizes = mesh.shape["dp"], mesh.shape["ctx"]
    return jax.shard_map(
        functools.partial(per_device, *sizes), mesh=mesh, in_specs=placed, out_specs=P("dp", "ctx", None), check_vma=False
    )
```

time: 172 us -> 71.8 us (0.42)
  waiting for transfers between devices: 99.9 us -> 0 us
  Pallas kernels: 0 us -> 68.4 us
  matrix products: 23.1 us -> 0 us
  between operations: 14.1 us -> 0.03 us
  local copies, waits for them, and re-layouts: 16.7 us -> 3.2 us
  other arithmetic: 12 us -> 0 us
  blocking collectives: 5.31 us -> 0 us
    all_gather x2 -> x0, waiting for transfers between devices: 99.2 us -> none  [the longest x1 82.9 us: per_device(): lax.all_gather(w_down, ('dp', 'ctx'), axis=0, tiled=True)]
    pallas_call x0 -> x2, Pallas kernels: none -> 68.4 us  [the longest x1 56.1 us: gather_latent(): pl.pallas_call(functools.partial(latent_kernel, layers), out_shape=[jax.S...]
    dot_general x9 -> x0, matrix products: 23.1 us -> none  [the longest x4 8.83 us: update(): jnp.einsum('kgsd,tkd->kgst', query_heads, key_block, preferred_element_ty...]
    unnamed x1 -> x0, blocking collectives: 5.31 us -> none
    add x9 -> x0, other arithmetic: 5.22 us -> none  [the longest x4 5.15 us: per_device(): jnp.where(local_ids < half_rows, block_order[0, 0], block_order[0, 1])]
    dynamic_slice x12 -> x0, local copies, waits for them, and re-layouts: 5.19 us -> none  [per_device(): result, unused = lax.scan(step_block, start_state, (blocks, key_positions))]
    while x20 -> x0, local copies, waits for them, and re-layouts: 5.18 us -> none
    reduce_sum x5 -> x0, other arithmetic: 4.37 us -> none  [the longest x4 4.29 us: update(): new_total = running_total * correction + jnp.sum(expo, axis=-1)]
  transfers between devices with their start and end apart: 2 -> 0, of which waited for: 2 -> 0; matrix products, arithmetic and copies ran while one was open for 3% -> 0% of each run, Pallas kernels for 0% -> 0%
where the time goes in v1:
time: 71.8 us; the launch traced here: 71.6 us
  Pallas kernels  68.4 us (95%)
  local copies, waits for them, and re-layouts  3.2 us (4%)
    pallas_call x1, Pallas kernels, gather_latent(): pl.pallas_call(functools.partial(latent_kernel, layers), out_shape=[jax.S...  56.1 us
    pallas_call x1, Pallas kernels, attend(): pl.pallas_call(attention_kernel, out_shape=jax.ShapeDtypeStruct(queries.s...  12.2 us
    unnamed x10, local copies, waits for them, and re-layouts  3.2 us

profile of v1, /device:TPU:1, one launch (start us, length us, event | category | flops | bytes accessed | tf_op | source)
XLA Modules:
  0.0 71.6 jit_solution(3611717226198295168)
XLA Ops:
  0.0 0.0 copy-start
  0.0 1.6 %copy-done = bf16[1,128,8192]{2,1,0:T(8,128)(2,1)S(1)} copy-done((bf16[1,128,8192]{2,1,0:T(8,128)(2,1)S(1)}, bf16[1,128,8192]{2,1,0:T(8,128)(2,1)}, u32[]{:S(2)}) %copy-start) | copy-done | bytes 2097176
  1.6 0.0 copy-start.3
  1.6 0.9 %copy-done.3 = bf16[256,512]{1,0:T(8,128)(2,1)S(1)} copy-done((bf16[256,512]{1,0:T(8,128)(2,1)S(1)}, bf16[256,512]{1,0:T(8,128)(2,1)}, u32[]{:S(2)}) %copy-start.3) | copy-done | bytes 262168
  2.5 0.0 copy-start.4
  2.5 0.7 copy-done.4
  3.2 0.0 copy-start.1
  3.2 0.0 copy-start.2
  3.2 56.1 %latent.1 = (bf16[1024,512]{1,0:T(8,128)(2,1)S(1)}, s32[8,1024]{1,0:T(8,128)S(1)}) custom-call(s32[1,2]{1,0:T(1,128)S(1)} %copy-done.4, bf16[1,128,8192]{2,1,0:T(8,128)(2,1)S(1)} %copy-done, bf16[256,512]{1,0:T(8,128)(2,1)S(1)} %copy-done.3), custom_call_target="tpu_custom_call" | custom-call | tf_op jit(solution)/shard_map/latent/pallas_call | solution.py:354
  59.4 0.0 copy-done.1
  59.4 0.0 copy-done.2
  59.4 12.2 %attention.1 = bf16[1,128,4096]{2,1,0:T(8,128)(2,1)} custom-call(s32[1,2]{1,0:T(1,128)S(1)} %copy-done.4, s32[8,1024]{1,0:T(8,128)S(1)} %get-tuple-element.7.pos_ref, bf16[1024,512]{1,0:T(8,128)(2,1)S(1)} %get-tuple-element.8.latent_ref, bf16[512,1024]{1,0:T(8,128)(2,1)S(1)} %copy-done.1, bf16[1,128,4096]{2,1,0:T(8,128)(2,1)S(1)} %copy-done.2), custom_call_target="tpu_custom_call" | custom-call | tf_op jit(solution)/shard_map/attention/pallas_call | solution.py:76
Async XLA Ops:
  0.0 1.6 %copy-start = (bf16[1,128,8192]{2,1,0:T(8,128)(2,1)S(1)}, bf16[1,128,8192]{2,1,0:T(8,128)(2,1)}, u32[]{:S(2)}) copy-start(bf16[1,128,8192]{2,1,0:T(8,128)(2,1)} %tokens_ref.1) | copy-start | bytes 6291460
  1.6 0.9 %copy-start.3 = (bf16[256,512]{1,0:T(8,128)(2,1)S(1)}, bf16[256,512]{1,0:T(8,128)(2,1)}, u32[]{:S(2)}) copy-start(bf16[256,512]{1,0:T(8,128)(2,1)} %w_ref.1) | copy-start | bytes 786436
  2.5 0.7 copy-start.4
  3.2 56.2 %copy-start.1 = (bf16[512,1024]{1,0:T(8,128)(2,1)S(1)}, bf16[512,1024]{1,0:T(8,128)(2,1)}, u32[]{:S(2)}) copy-start(bf16[512,1024]{1,0:T(8,128)(2,1)} %w_up_ref.1) | copy-start | bytes 3145732
  3.2 56.2 %copy-start.2 = (bf16[1,128,4096]{2,1,0:T(8,128)(2,1)S(1)}, bf16[1,128,4096]{2,1,0:T(8,128)(2,1)}, u32[]{:S(2)}) copy-start(bf16[1,128,4096]{2,1,0:T(8,128)(2,1)} %q_ref.1) | copy-start | bytes 3145732

commit v2 on v1

--- a/solution.py
+++ b/solution.py
@@ -85,6 +85,19 @@
         compiler_params=pltpu.CompilerParams(vmem_limit_bytes=48 * 2**20),
         name="attention",
     )(block_order, positions, latent, w_up, queries)
+
+
+def order(layers):
+    steps = [("a", 0, 0), ("c", 1, 0), ("a", 0, 1), ("c", 1, 1), ("z", 0, 0), ("z", 0, 1)]
+    for t in range(1, layers):
+        if t + 1 < layers:
+            steps += [("c", t + 1, 0), ("c", t + 1, 1)]
+        if t > 1:
+            steps += [("z", t - 1, 0), ("z", t - 1, 1), ("A", t - 2)]
+        steps += [("C", t), ("a", t, 0), ("a", t, 1)]
+    steps += [("Z", t) for t in range(layers - 2)] + [("A", layers - 2)]
+    steps += [("z", layers - 1, 0), ("z", layers - 1, 1), ("A", layers - 1), ("Z", layers - 2), ("Z", layers - 1)]
+    return steps
 
 
 def latent_kernel(
@@ -181,44 +194,59 @@
     def piece(j, q):
         return w.at[j, pl.ds(q * quarter, quarter), :]
 
-    def column(t):
+    def side(j, h):
+        return w.at[j, pl.ds(h * 2 * quarter, 2 * quarter), :]
+
+    def column(t, h):
         for s, layer, conds in sources(t):
             j = layer * 4 + p
-            block = w_ref if t == 0 else w.at[j]
+            block = w_ref.at[pl.ds(h * 2 * quarter, 2 * quarter), :] if t == 0 else side(j, h)
             if t:
-                when(conds, lambda: arrived(w.at[j], w_recv.at[j]))
+                when(conds, lambda: arrived(side(j, h), w_recv.at[j, h]))
             for step in ahead(s):
-                send(conds + [inside(z + step)], block, w.at[j], w_recv.at[j], (z + step, ctx))
-            send(conds, block, w.at[j], w_recv.at[j], (z, x_dev))
-            send(conds, block, w.at[j], w_recv.at[j], (z, y_dev))
-            if t:
-                when(conds, lambda: multiply(j))
-
-    def sides(t):
-        for s, layer, conds in sources(t):
-            for place, device, first in ((px, y_dev, 0), (py, x_dev, 1)):
+                send(conds + [inside(z + step)], block, side(j, h), w_recv.at[j, h], (z + step, ctx))
+            for device in (x_dev, y_dev):
+                send(conds, block, side(j, h), w_recv.at[j, h], (z, device))
+
+    def across(t, h):
+        place, device = ((px, y_dev), (py, x_dev))[h]
+        for s, layer, conds in sources(t):
+            j = layer * 4 + place
+            when(conds, lambda: arrived(side(j, h), w_recv.at[j, h]))
+            for q in (2 * h + 1, 2 * h) if t == 0 else (2 * h,):
+                send(conds, piece(j, q), piece(j, q), piece_recv.at[layer, q], (z, device))
+
+    def corner(t, h):
+        q = 2 * h + 1
+        for s, layer, conds in sources(t):
+            j = layer * 4 + pd
+            when(conds, lambda: arrived(piece(j, q), piece_recv.at[layer, q]))
+            for step in ahead(s):
+                send(
+                    conds + [inside(z + step)], piece(j, q), piece(j, q), piece_recv.at[layer, q], (z + step, ctx)
+                )
+
+    def finish_column(t):
+        for s, layer, conds in sources(t):
+            when(conds, lambda: multiply(layer * 4 + p))
+
+    def finish_across(t):
+        for s, layer, conds in sources(t):
+            for place, h in ((px, 1), (py, 0)):
                 j = layer * 4 + place
-                when(conds, lambda: arrived(w.at[j], w_recv.at[j]))
-                for q in (first + 2, first) if t == 0 else (first,):
-                    send(conds, piece(j, q), piece(j, q), piece_recv.at[layer, q], (z, device))
+                when(conds, lambda: arrived(side(j, h), w_recv.at[j, h]))
             for place in (px, py):
                 when(conds, lambda: multiply(layer * 4 + place))
 
-    def corner(t):
+    def finish_corner(t):
         for s, layer, conds in sources(t):
             j = layer * 4 + pd
-            for q in (2, 3):
-                when(conds, lambda: arrived(piece(j, q), piece_recv.at[layer, q]))
-                for step in ahead(s):
-                    send(
-                        conds + [inside(z + step)], piece(j, q), piece(j, q), piece_recv.at[layer, q],
-                        (z + step, ctx),
-                    )
-            for q in (0, 1):
+            for q in (0, 2):
                 when(conds, lambda: arrived(piece(j, q), piece_recv.at[layer, q]))
             when(conds, lambda: multiply(j))
 
-    column(0)
+    column(0, 0)
+    column(0, 1)
 
     def start_tokens(j, unused):
         swap(j).start()
@@ -253,13 +281,11 @@
     own_load.wait()
     acc[...] = jnp.dot(tok[own], w[own], preferred_element_type=jnp.float32)
 
-    for t in range(layers + 2):
-        if 1 <= t < layers:
-            column(t)
-        if 0 <= t - 1 < layers:
-            sides(t - 1)
-        if 0 <= t - 2 < layers:
-            corner(t - 2)
+    steps = dict(
+        c=column, a=across, z=corner, C=finish_column, A=finish_across, Z=finish_corner
+    )
+    for kind, *where in order(layers):
+        steps[kind](*where)
 
     total = pltpu.make_async_remote_copy(
         acc.at[pl.ds(rows, rows), :], share, sum_sem.at[0], sum_sem.at[1],
@@ -312,16 +338,21 @@
         return device + 1 - 2 * core
 
     d_dev = pd * 2 + core
-    lat_send_to(mine, block(ctx), 0, x_dev)
-    lat_send_to(mine, block(ctx), 1, y_dev)
+    low, high = pl.ds(0, part), pl.ds(part, part)
+    lat_send_to(mine.at[low], block(ctx, 0, part), 0, x_dev)
+    lat_send_to(mine.at[high], block(ctx, part, part), 1, y_dev)
+    lat_send_to(mine.at[high], block(ctx, part, part), 9, x_dev)
+    lat_send_to(mine.at[low], block(ctx, 0, part), 10, y_dev)
     lat_send_to(mine, block(ctx), 2, mate)
     store(mine, ctx, 0)
-    lat_arrived(block(x_dev), 0)
+    lat_arrived(block(x_dev, 0, part), 0)
     lat_send_to(block(x_dev, 0, part), block(x_dev, 0, part), 3, y_dev)
+    lat_arrived(block(y_dev, part, part), 1)
+    lat_send_to(block(y_dev, part, part), block(y_dev, part, part), 4, x_dev)
+    lat_arrived(block(x_dev, part, part), 9)
     lat_send_to(block(x_dev), block(x_dev), 5, mate)
     store(block(x_dev), x_dev, 1)
-    lat_arrived(block(y_dev), 1)
-    lat_send_to(block(y_dev, part, part), block(y_dev, part, part), 4, x_dev)
+    lat_arrived(block(y_dev, 0, part), 10)
     lat_send_to(block(y_dev), block(y_dev), 6, mate)
     store(block(y_dev), y_dev, 2)
     lat_arrived(block(mate), 2)
@@ -350,7 +381,7 @@
     depth, width = w_down.shape
     chunks = layers * 4
     dma = pltpu.SemaphoreType.DMA
-    whole = pl.BlockSpec(memory_space=pl.ANY)
+    whole = pl.BlockSpec(memory_space=pltpu.HBM)
     return pl.pallas_call(
         functools.partial(latent_kernel, layers),
         out_shape=[
@@ -372,14 +403,14 @@
             dma,
             dma((chunks,)),
             dma((chunks,)),
-            dma((96,)),
-            dma((chunks,)),
+            dma((160,)),
+            dma((chunks, 2)),
             dma((layers, 4)),
             dma((8,)),
             dma((8,)),
             dma((2,)),
-            dma((10,)),
-            dma((9,)),
+            dma((12,)),
+            dma((11,)),
             dma((9,)),
         ],
         compiler_params=pltpu.CompilerParams(
@@ -392,7 +423,7 @@
 def per_device(layers, plane, tokens, w_down, w_up, queries, block_order):
     local_rows = tokens.shape[1]
     half_rows = local_rows // 2
-    if plane == 8:
+    if plane == 8 and layers > 1:
         latent, positions = gather_latent(layers, tokens, w_down, block_order)
         return attend(block_order, positions, latent, w_up, queries)
     summed = jnp.dot(

time: 71.8 us -> 66.2 us (0.922)
  Pallas kernels: 68.4 us -> 62.8 us
    pallas_call x1, Pallas kernels: 56.1 us -> 50.6 us  [gather_latent(): pl.pallas_call(functools.partial(latent_kernel, layers), out_shape=[jax.S...]
where the time goes in v2:
time: 66.2 us; the launch traced here: 66 us
  Pallas kernels  62.8 us (95%)
  local copies, waits for them, and re-layouts  3.2 us (5%)
    pallas_call x1, Pallas kernels, gather_latent(): pl.pallas_call(functools.partial(latent_kernel, layers), out_shape=[jax.S...  50.6 us
    pallas_call x1, Pallas kernels, attend(): pl.pallas_call(attention_kernel, out_shape=jax.ShapeDtypeStruct(queries.s...  12.2 us
    unnamed x10, local copies, waits for them, and re-layouts  3.2 us

profile of v2, /device:TPU:1, one launch (start us, length us, event | category | flops | bytes accessed | tf_op | source)
XLA Modules:
  0.0 66.0 jit_solution(3970274678602014051)
XLA Ops:
  0.0 0.0 copy-start
  0.0 1.6 %copy-done = bf16[1,128,8192]{2,1,0:T(8,128)(2,1)S(1)} copy-done((bf16[1,128,8192]{2,1,0:T(8,128)(2,1)S(1)}, bf16[1,128,8192]{2,1,0:T(8,128)(2,1)}, u32[]{:S(2)}) %copy-start) | copy-done | bytes 2097176
  1.6 0.0 copy-start.3
  1.6 0.9 %copy-done.3 = bf16[256,512]{1,0:T(8,128)(2,1)S(1)} copy-done((bf16[256,512]{1,0:T(8,128)(2,1)S(1)}, bf16[256,512]{1,0:T(8,128)(2,1)}, u32[]{:S(2)}) %copy-start.3) | copy-done | bytes 262168
  2.5 0.0 copy-start.4
  2.5 0.7 copy-done.4
  3.2 0.0 copy-start.1
  3.2 0.0 copy-start.2
  3.2 50.6 %latent.1 = (bf16[1024,512]{1,0:T(8,128)(2,1)S(1)}, s32[8,1024]{1,0:T(8,128)S(1)}) custom-call(s32[1,2]{1,0:T(1,128)S(1)} %copy-done.4, bf16[1,128,8192]{2,1,0:T(8,128)(2,1)S(1)} %copy-done, bf16[256,512]{1,0:T(8,128)(2,1)S(1)} %copy-done.3), custom_call_target="tpu_custom_call" | custom-call | tf_op jit(solution)/shard_map/latent/pallas_call | solution.py:385
  53.8 0.0 copy-done.1
  53.8 0.0 copy-done.2
  53.8 12.2 %attention.1 = bf16[1,128,4096]{2,1,0:T(8,128)(2,1)} custom-call(s32[1,2]{1,0:T(1,128)S(1)} %copy-done.4, s32[8,1024]{1,0:T(8,128)S(1)} %get-tuple-element.7.pos_ref, bf16[1024,512]{1,0:T(8,128)(2,1)S(1)} %get-tuple-element.8.latent_ref, bf16[512,1024]{1,0:T(8,128)(2,1)S(1)} %copy-done.1, bf16[1,128,4096]{2,1,0:T(8,128)(2,1)S(1)} %copy-done.2), custom_call_target="tpu_custom_call" | custom-call | tf_op jit(solution)/shard_map/attention/pallas_call | solution.py:76
Async XLA Ops:
  0.0 1.6 %copy-start = (bf16[1,128,8192]{2,1,0:T(8,128)(2,1)S(1)}, bf16[1,128,8192]{2,1,0:T(8,128)(2,1)}, u32[]{:S(2)}) copy-start(bf16[1,128,8192]{2,1,0:T(8,128)(2,1)} %tokens_ref.1) | copy-start | bytes 6291460
  1.6 0.9 %copy-start.3 = (bf16[256,512]{1,0:T(8,128)(2,1)S(1)}, bf16[256,512]{1,0:T(8,128)(2,1)}, u32[]{:S(2)}) copy-start(bf16[256,512]{1,0:T(8,128)(2,1)} %w_ref.1) | copy-start | bytes 786436
  2.5 0.7 copy-start.4
  3.2 50.6 %copy-start.1 = (bf16[512,1024]{1,0:T(8,128)(2,1)S(1)}, bf16[512,1024]{1,0:T(8,128)(2,1)}, u32[]{:S(2)}) copy-start(bf16[512,1024]{1,0:T(8,128)(2,1)} %w_up_ref.1) | copy-start | bytes 3145732
  3.2 50.6 %copy-start.2 = (bf16[1,128,4096]{2,1,0:T(8,128)(2,1)S(1)}, bf16[1,128,4096]{2,1,0:T(8,128)(2,1)}, u32[]{:S(2)}) copy-start(bf16[1,128,4096]{2,1,0:T(8,128)(2,1)} %q_ref.1) | copy-start | bytes 3145732

commit v3 on v2

--- a/solution.py
+++ b/solution.py
@@ -34,39 +34,49 @@
     heads = 2
     group = QH // KVH
 
-    def step(i):
-        def cols(first, width):
-            return pl.ds(pl.multiple_of(first * HD, HD), width * HD)
-
-        g = i * heads // group
+    def cols(first, width):
+        return pl.ds(pl.multiple_of(first * HD, HD), width * HD)
+
+    def score(i):
         queries = jnp.concatenate(
             [q_ref[0, :, cols(i * heads + k, 1)] for k in range(heads)], axis=0
         )
-        scores = lax.dot_general(
-            queries, kv[:, cols(g, 1)], (((1,), (1,)), ((), ())), preferred_element_type=jnp.float32
-        )
+        return lax.dot_general(
+            queries,
+            kv[:, cols(i * heads // group, 1)],
+            (((1,), (1,)), ((), ())),
+            preferred_element_type=jnp.float32,
+        )
+
+    def weigh(i, scores):
         parts, totals = [], []
-        for k in range(heads):
-            kept = scores[k * rows : (k + 1) * rows] * scale + bias[...]
+        for first in range(0, heads * rows, strip):
+            own = first % rows
+            kept = scores[first : first + strip] * scale + bias[own : own + strip]
             largest = jnp.max(kept, axis=1, keepdims=True)
             expo = jnp.exp2(kept - largest)
             totals.append(jnp.sum(expo, axis=1, keepdims=True))
             parts.append(expo.astype(jnp.bfloat16))
         summed = jnp.dot(
-            jnp.concatenate(parts, axis=0), kv[:, cols(KVH + g, 1)], preferred_element_type=jnp.float32
-        )
+            jnp.concatenate(parts, axis=0),
+            kv[:, cols(KVH + i * heads // group, 1)],
+            preferred_element_type=jnp.float32,
+        )
+        summed = (summed / jnp.concatenate(totals, axis=0)).astype(jnp.bfloat16)
         for k in range(heads):
-            out_ref[0, :, cols(i * heads + k, 1)] = (
-                summed[k * rows : (k + 1) * rows] / totals[k]
-            ).astype(jnp.bfloat16)
+            out_ref[0, :, cols(i * heads + k, 1)] = summed[k * rows : (k + 1) * rows]
 
     pairs = QH // heads
-    together = 4 if count <= 1024 else 1
+    together = 16 if count <= 1024 else 1
+    strip = 16
 
     @pl.loop(0, pairs // together)
     def _(i):
+        scores = score(i * together)
         for k in range(together):
-            step(i * together + k)
+            ahead = score(i * together + k + 1) if k + 1 < together else None
+            weigh(i * together + k, scores)
+            scores = ahead
 
 
 def attend(block_order, positions, latent, w_up, queries):

time: 66.2 us -> 64.4 us (0.973)
  Pallas kernels: 62.8 us -> 61 us
    pallas_call x1, Pallas kernels: 12.2 us -> 10.5 us  [attend(): pl.pallas_call(attention_kernel, out_shape=jax.ShapeDtypeStruct(queries.s...]
where the time goes in v3:
time: 64.4 us; the launch traced here: 64.3 us
  Pallas kernels  61 us (95%)
  local copies, waits for them, and re-layouts  3.2 us (5%)
    pallas_call x1, Pallas kernels, gather_latent(): pl.pallas_call(functools.partial(latent_kernel, layers), out_shape=[jax.S...  50.6 us
    pallas_call x1, Pallas kernels, attend(): pl.pallas_call(attention_kernel, out_shape=jax.ShapeDtypeStruct(queries.s...  10.5 us
    unnamed x10, local copies, waits for them, and re-layouts  3.2 us

profile of v3, /device:TPU:1, one launch (start us, length us, event | category | flops | bytes accessed | tf_op | source)
XLA Modules:
  0.0 64.3 jit_solution(13959184346237867613)
XLA Ops:
  0.0 0.0 copy-start
  0.0 1.6 %copy-done = bf16[1,128,8192]{2,1,0:T(8,128)(2,1)S(1)} copy-done((bf16[1,128,8192]{2,1,0:T(8,128)(2,1)S(1)}, bf16[1,128,8192]{2,1,0:T(8,128)(2,1)}, u32[]{:S(2)}) %copy-start) | copy-done | bytes 2097176
  1.6 0.0 copy-start.3
  1.6 0.9 %copy-done.3 = bf16[256,512]{1,0:T(8,128)(2,1)S(1)} copy-done((bf16[256,512]{1,0:T(8,128)(2,1)S(1)}, bf16[256,512]{1,0:T(8,128)(2,1)}, u32[]{:S(2)}) %copy-start.3) | copy-done | bytes 262168
  2.5 0.0 copy-start.4
  2.5 0.7 %copy-done.4 = s32[1,2]{1,0:T(1,128)S(1)} copy-done((s32[1,2]{1,0:T(1,128)S(1)}, s32[1,2]{1,0:T(1,128)}, u32[]{:S(2)}) %copy-start.4) | copy-done | bytes 32
  3.2 0.0 copy-start.1
  3.2 0.0 copy-start.2
  3.2 50.6 %latent.1 = (bf16[1024,512]{1,0:T(8,128)(2,1)S(1)}, s32[8,1024]{1,0:T(8,128)S(1)}) custom-call(s32[1,2]{1,0:T(1,128)S(1)} %copy-done.4, bf16[1,128,8192]{2,1,0:T(8,128)(2,1)S(1)} %copy-done, bf16[256,512]{1,0:T(8,128)(2,1)S(1)} %copy-done.3), custom_call_target="tpu_custom_call" | custom-call | tf_op jit(solution)/shard_map/latent/pallas_call | solution.py:395
  53.8 0.0 copy-done.1
  53.8 0.0 copy-done.2
  53.8 10.5 %attention.1 = bf16[1,128,4096]{2,1,0:T(8,128)(2,1)} custom-call(s32[1,2]{1,0:T(1,128)S(1)} %copy-done.4, s32[8,1024]{1,0:T(8,128)S(1)} %get-tuple-element.7.pos_ref, bf16[1024,512]{1,0:T(8,128)(2,1)S(1)} %get-tuple-element.8.latent_ref, bf16[512,1024]{1,0:T(8,128)(2,1)S(1)} %copy-done.1, bf16[1,128,4096]{2,1,0:T(8,128)(2,1)S(1)} %copy-done.2), custom_call_target="tpu_custom_call" | custom-call | tf_op jit(solution)/shard_map/attention/pallas_call | solution.py:86
Async XLA Ops:
  0.0 1.6 %copy-start = (bf16[1,128,8192]{2,1,0:T(8,128)(2,1)S(1)}, bf16[1,128,8192]{2,1,0:T(8,128)(2,1)}, u32[]{:S(2)}) copy-start(bf16[1,128,8192]{2,1,0:T(8,128)(2,1)} %tokens_ref.1) | copy-start | bytes 6291460
  1.6 0.9 %copy-start.3 = (bf16[256,512]{1,0:T(8,128)(2,1)S(1)}, bf16[256,512]{1,0:T(8,128)(2,1)}, u32[]{:S(2)}) copy-start(bf16[256,512]{1,0:T(8,128)(2,1)} %w_ref.1) | copy-start | bytes 786436
  2.5 0.7 %copy-start.4 = (s32[1,2]{1,0:T(1,128)S(1)}, s32[1,2]{1,0:T(1,128)}, u32[]{:S(2)}) copy-start(s32[1,2]{1,0:T(1,128)} %order_ref.3) | copy-start | bytes 28
  3.2 50.6 %copy-start.1 = (bf16[512,1024]{1,0:T(8,128)(2,1)S(1)}, bf16[512,1024]{1,0:T(8,128)(2,1)}, u32[]{:S(2)}) copy-start(bf16[512,1024]{1,0:T(8,128)(2,1)} %w_up_ref.1) | copy-start | bytes 3145732
  3.2 50.6 %copy-start.2 = (bf16[1,128,4096]{2,1,0:T(8,128)(2,1)S(1)}, bf16[1,128,4096]{2,1,0:T(8,128)(2,1)}, u32[]{:S(2)}) copy-start(bf16[1,128,4096]{2,1,0:T(8,128)(2,1)} %q_ref.1) | copy-start | bytes 3145732

commit v4 on v3

--- a/solution.py
+++ b/solution.py
@@ -92,7 +92,7 @@
             pltpu.VMEM((count, w_up.shape[1]), jnp.bfloat16),
             pltpu.VMEM((rows, count), jnp.float32),
         ],
-        compiler_params=pltpu.CompilerParams(vmem_limit_bytes=48 * 2**20),
+        compiler_params=pltpu.CompilerParams(vmem_limit_bytes=60 * 2**20),
         name="attention",
     )(block_order, positions, latent, w_up, queries)
 
@@ -424,7 +424,7 @@
             dma((9,)),
         ],
         compiler_params=pltpu.CompilerParams(
-            collective_id=0, has_side_effects=True, vmem_limit_bytes=48 * 2**20
+            collective_id=0, has_side_effects=True, vmem_limit_bytes=60 * 2**20
         ),
         name="latent",
     )(block_order, tokens, w_down)

time: 64.4 us -> 63.4 us (0.984)
  local copies, waits for them, and re-layouts: 3.2 us -> 0 us
  Pallas kernels: 61 us -> 63.2 us
    unnamed x10 -> x0, local copies, waits for them, and re-layouts: 3.2 us -> none
    pallas_call x1, Pallas kernels: 10.5 us -> 11.7 us  [attend(): pl.pallas_call(attention_kernel, out_shape=jax.ShapeDtypeStruct(queries.s...]
    pallas_call x1, Pallas kernels: 50.6 us -> 51.4 us  [gather_latent(): pl.pallas_call(functools.partial(latent_kernel, layers), out_shape=[jax.S...]
where the time goes in v4:
time: 63.4 us; the launch traced here: 63.2 us
  Pallas kernels  63.2 us (100%)
    pallas_call x1, Pallas kernels, gather_latent(): pl.pallas_call(functools.partial(latent_kernel, layers), out_shape=[jax.S...  51.4 us
    pallas_call x1, Pallas kernels, attend(): pl.pallas_call(attention_kernel, out_shape=jax.ShapeDtypeStruct(queries.s...  11.7 us

profile of v4, /device:TPU:1, one launch (start us, length us, event | category | flops | bytes accessed | tf_op | source)
XLA Modules:
  0.0 63.2 jit_solution(4235987055767814391)
XLA Ops:
  0.0 51.4 %latent.1 = (bf16[1024,512]{1,0:T(8,128)(2,1)}, s32[8,1024]{1,0:T(8,128)}) custom-call(s32[1,2]{1,0:T(1,128)} %order_ref.3, bf16[1,128,8192]{2,1,0:T(8,128)(2,1)} %tokens_ref.1, bf16[256,512]{1,0:T(8,128)(2,1)} %w_ref.1), custom_call_target="tpu_custom_call" | custom-call | tf_op jit(solution)/shard_map/latent/pallas_call | solution.py:395
  51.4 11.7 %attention.1 = bf16[1,128,4096]{2,1,0:T(8,128)(2,1)} custom-call(s32[1,2]{1,0:T(1,128)} %order_ref.3, s32[8,1024]{1,0:T(8,128)} %get-tuple-element.7.pos_ref, bf16[1024,512]{1,0:T(8,128)(2,1)} %get-tuple-element.8.latent_ref, bf16[512,1024]{1,0:T(8,128)(2,1)} %w_up_ref.1, bf16[1,128,4096]{2,1,0:T(8,128)(2,1)} %q_ref.1), custom_call_target="tpu_custom_call" | custom-call | tf_op jit(solution)/shard_map/attention/pallas_call | solution.py:86
